TPU v7x, 256 devices: a whole 4x4x8 slice. The times are simulated.
256 devices in a mesh: wide: 64 (over z_hi, x, y, core), narrow: 4 (over z_lo).
Axes of the slice: x: 4, y: 4, z: 8 (z_hi: 2, z_lo: 4; z = z_hi * 4 + z_lo), core: 2. Of those that a mesh axis runs over, the one named last changes fastest.
Arguments:
- factor_rows: float32 [1, 4, 4, 64, 16, 1024], P(None, 'narrow', None, 'wide'), may hold values from -0.09375 to 0.09375
- load_vectors: float32 [1, 4, 1024, 128], P(None, 'narrow', 'wide'), may hold values from -6 to 6
- child_updates: float32 [4, 1, 4, 1024, 128], P('narrow', None, None, 'wide'), may hold values from -4 to 4
- block_inverses: float32 [4, 1024, 1024], P(None, 'wide'), may hold values from -1 to 2, as said below
Outputs:
- forward_solution: float32 [1, 4, 1024, 128], P(None, 'narrow', 'wide')
Inputs may be any that keep to these rules, and one draw needn't show every extreme that they name: Each block of block_inverses has a diagonal between 0.4 and 1.6.
All inputs are finite; a program needn't handle non-finite values.
Results may differ from a plain program's by a relative error of at most 0.0001.
Values sent between devices are 32-bit elements; how exact they have to be, the bound alone decides.
A program may use at most 64 MiB of HBM per device.

v0:
```python
import jax
import jax.numpy as jnp
from jax import lax
from jax.sharding import PartitionSpec as P


def from_root(shard, axis, root):
    mine = lax.axis_index(axis) == root
    return lax.psum(jnp.where(mine, shard, jnp.zeros_like(shard)), axis)


def body(factor_rows, load_vectors, child_updates, block_inverses):
    blocks_dev = factor_rows.shape[0]
    narrow_count = lax.axis_size("narrow")
    block_count = blocks_dev * narrow_count
    sub_rows = factor_rows.shape[4]
    block_width = factor_rows.shape[5]
    case_count = load_vectors.shape[3]
    my_lane = lax.axis_index("narrow")
    panel = factor_rows.reshape(blocks_dev, block_count, sub_rows, block_width)
    kid_sums = lax.psum_scatter(child_updates, "narrow", scatter_dimension=2, tiled=True)
    given_part = load_vectors.reshape(blocks_dev, sub_rows, case_count) - kid_sums.reshape(
        blocks_dev, sub_rows, case_count
    )
    solved = jnp.zeros((block_count, sub_rows, case_count), jnp.float32)
    held_sums = jnp.zeros((blocks_dev, block_width, case_count), jnp.float32)

    def advance(block_index, state_pair):
        solved, held_sums = state_pair
        own_block = block_index // narrow_count
        owner = block_index % narrow_count
        rows_here = lax.dynamic_index_in_dim(panel, own_block, 0, keepdims=False)
        reduced = lax.psum_scatter(
            jnp.einsum("cqr,cqk->rk", rows_here, solved, precision=lax.Precision.HIGHEST),
            "wide",
            scatter_dimension=0,
            tiled=True,
        )
        residual_part = lax.dynamic_index_in_dim(given_part, own_block, 0, keepdims=False) - reduced
        inverse_rows = lax.dynamic_index_in_dim(block_inverses, block_index, 0, keepdims=False)
        residual_full = lax.all_gather(residual_part, "wide", axis=0, tiled=True)
        applied = jnp.dot(
            inverse_rows,
            residual_full,
            precision=lax.Precision.HIGHEST,
            preferred_element_type=jnp.float32,
        )
        newest = from_root(applied, "narrow", owner)
        solved = lax.dynamic_update_index_in_dim(solved, newest, block_index, 0)
        return (solved, held_sums)

    solved, held_sums = lax.fori_loop(0, block_count, advance, (solved, held_sums))
    arranged = solved.reshape(blocks_dev, narrow_count, sub_rows, case_count)
    return lax.dynamic_slice_in_dim(arranged, my_lane, 1, 1)


def solution(mesh):
    placed = (
        P(None, "narrow", None, "wide", None, None),
        P(None, "narrow", "wide", None),
        P("narrow", None, None, "wide", None),
        P(None, "wide", None),
    )
    return jax.shard_map(
        body, mesh=mesh, in_specs=placed, out_specs=P(None, "narrow", "wide", None), check_vma=False
    )
```

profile of v0, /device:TPU:8, one launch (start us, length us, event | category | flops | bytes accessed | tf_op | source)
XLA Modules:
  0.0 2172.6 jit_solution(16757187029783483254)
XLA Ops:
  6.5 0.7 reduce-scatter.3.cloned.1.call-update
  7.3 29.7 %reduce-scatter.3.cloned.1.call-done = f32[1,1,1,16,128]{4,3,2,1,0:T(8,128)} async-done(((f32[1,1,4,16,128]{4,3,2,1,0:T(8,128)}), f32[1,1,1,16,128]{4,3,2,1,0:T(8,128)}) %reduce-scatter.3.cloned.1.call-update) | async-done | bytes 8208 | tf_op jit(solution)/shard_map/reduce_scatter | solution.py:21
  36.9 0.7 bitcast_subtract_fusion.1
  37.6 2127.8 %while.15 = (s32[]{:T(128)}, f32[4,16,128]{2,1,0:T(8,128)S(1)}, f32[4,16,1024]{2,1,0:T(8,128)}, f32[1,16,128]{2,1,0:T(8,128)S(1)}, f32[1,4,16,1024]{3,2,1,0:T(8,...) while((s32[]{:T(128)}, f32[4,16,128]{2,1,0:T(8,128)S(1)}, f32[4,16,1024]{2,1,0:T(8,128)}, ...), condition=%wide.region_4.5_spmd, body=%wide.region_1.4_spmd.sunk | while | flops 125835264 | bytes 3604725 | solution.py:52
  37.7 2.7 convolution_bitcast_fusion.2
  40.4 401.7 %reduce-scatter.5.cloned.1.call-done = f32[16,128]{1,0:T(8,128)} async-done(((f32[1024,128]{1,0:T(8,128)}), f32[16,128]{1,0:T(8,128)}) %reduce-scatter.5.cloned.1.call-update) | async-done | bytes 8208 | tf_op jit(solution)/shard_map/while/body/eval_jaxpr/reduce_scatter | solution.py:33
  442.2 0.7 bitcast_subtract_fusion.3
  442.9 119.2 %all_gather.11 = f32[1024,128]{1,0:T(8,128)S(1)} all-gather(f32[16,128]{1,0:T(8,128)S(1)} %bitcast_subtract_fusion.3), channel_id=1, replica_groups=mesh['wide'=64,'narrow'=4] {'wide'}, dimensions={0}, use_global_device_ids=true | all-gather | bytes 532480 | tf_op jit(solution)/shard_map/while/body/eval_jaxpr/all_gather | solution.py:41
  562.0 1.2 fusion.16
  563.2 10.3 psum.15
  573.6 0.0 reduce-scatter.5.cloned.1.call-start
  573.6 2.7 convolution_bitcast_fusion.2
  576.4 397.5 %reduce-scatter.5.cloned.1.call-done = f32[16,128]{1,0:T(8,128)} async-done(((f32[1024,128]{1,0:T(8,128)}), f32[16,128]{1,0:T(8,128)}) %reduce-scatter.5.cloned.1.call-update) | async-done | bytes 8208 | tf_op jit(solution)/shard_map/while/body/eval_jaxpr/reduce_scatter | solution.py:33
  973.9 0.7 bitcast_subtract_fusion.3
  974.6 119.1 %all_gather.11 = f32[1024,128]{1,0:T(8,128)S(1)} all-gather(f32[16,128]{1,0:T(8,128)S(1)} %bitcast_subtract_fusion.3), channel_id=1, replica_groups=mesh['wide'=64,'narrow'=4] {'wide'}, dimensions={0}, use_global_device_ids=true | all-gather | bytes 532480 | tf_op jit(solution)/shard_map/while/body/eval_jaxpr/all_gather | solution.py:41
  1093.8 1.2 fusion.16
  1095.0 9.3 psum.15
  1104.4 0.0 reduce-scatter.5.cloned.1.call-start
  1104.4 2.7 convolution_bitcast_fusion.2
  1107.2 397.3 %reduce-scatter.5.cloned.1.call-done = f32[16,128]{1,0:T(8,128)} async-done(((f32[1024,128]{1,0:T(8,128)}), f32[16,128]{1,0:T(8,128)}) %reduce-scatter.5.cloned.1.call-update) | async-done | bytes 8208 | tf_op jit(solution)/shard_map/while/body/eval_jaxpr/reduce_scatter | solution.py:33
  1504.5 0.7 bitcast_subtract_fusion.3
  1505.2 119.1 %all_gather.11 = f32[1024,128]{1,0:T(8,128)S(1)} all-gather(f32[16,128]{1,0:T(8,128)S(1)} %bitcast_subtract_fusion.3), channel_id=1, replica_groups=mesh['wide'=64,'narrow'=4] {'wide'}, dimensions={0}, use_global_device_ids=true | all-gather | bytes 532480 | tf_op jit(solution)/shard_map/while/body/eval_jaxpr/all_gather | solution.py:41
  1624.3 1.2 fusion.16
  1625.5 9.4 psum.15
  1634.9 0.0 reduce-scatter.5.cloned.1.call-start
  1635.0 2.7 convolution_bitcast_fusion.2
  1637.7 397.3 %reduce-scatter.5.cloned.1.call-done = f32[16,128]{1,0:T(8,128)} async-done(((f32[1024,128]{1,0:T(8,128)}), f32[16,128]{1,0:T(8,128)}) %reduce-scatter.5.cloned.1.call-update) | async-done | bytes 8208 | tf_op jit(solution)/shard_map/while/body/eval_jaxpr/reduce_scatter | solution.py:33
  2035.0 0.7 bitcast_subtract_fusion.3
  2035.7 119.1 %all_gather.11 = f32[1024,128]{1,0:T(8,128)S(1)} all-gather(f32[16,128]{1,0:T(8,128)S(1)} %bitcast_subtract_fusion.3), channel_id=1, replica_groups=mesh['wide'=64,'narrow'=4] {'wide'}, dimensions={0}, use_global_device_ids=true | all-gather | bytes 532480 | tf_op jit(solution)/shard_map/while/body/eval_jaxpr/all_gather | solution.py:41
  2154.8 1.2 fusion.16
  2156.1 9.3 psum.15
  2165.4 0.6 dynamic-slice_bitcast_fusion
  (13 shorter events, 0.1 us)
Async XLA Ops:
  6.5 30.4 %reduce-scatter.3.cloned.1.call-start = ((), (), s32[]{:S(2)}) async-start(), calls=%async_computation.2 | async-start | bytes 40960 | tf_op jit(solution)/shard_map/reduce_scatter | solution.py:21
  7.3 29.7 %copy-start = (f32[1,1,16,128]{3,2,1,0:T(8,128)S(1)}, f32[1,1,16,128]{3,2,1,0:T(8,128)}, u32[]{:S(2)}) copy-start(f32[1,1,16,128]{3,2,1,0:T(8,128)} %param.7) | copy-start | bytes 24580
  37.6 404.5 %reduce-scatter.5.cloned.1.call-start = ((), (), s32[]{:S(2)}) async-start(), calls=%async_computation.3 | async-start | bytes 532480 | tf_op jit(solution)/shard_map/while/body/eval_jaxpr/reduce_scatter | solution.py:33
  573.6 400.3 %reduce-scatter.5.cloned.1.call-start = ((), (), s32[]{:S(2)}) async-start(), calls=%async_computation.3 | async-start | bytes 532480 | tf_op jit(solution)/shard_map/while/body/eval_jaxpr/reduce_scatter | solution.py:33
  1104.4 400.1 %reduce-scatter.5.cloned.1.call-start = ((), (), s32[]{:S(2)}) async-start(), calls=%async_computation.3 | async-start | bytes 532480 | tf_op jit(solution)/shard_map/while/body/eval_jaxpr/reduce_scatter | solution.py:33
  1634.9 400.1 %reduce-scatter.5.cloned.1.call-start = ((), (), s32[]{:S(2)}) async-start(), calls=%async_computation.3 | async-start | bytes 532480 | tf_op jit(solution)/shard_map/while/body/eval_jaxpr/reduce_scatter | solution.py:33
Sparse Core Ops, SparseCore 0:
  9.8 27.0 reduce-scatter.2
  41.1 400.9 reduce-scatter.4
  577.0 396.8 reduce-scatter.4
  1107.5 396.8 reduce-scatter.4
  1638.1 396.8 reduce-scatter.4
where the time goes:
time: 2170 us
  waiting for transfers between devices  1620 us (75%)
  blocking collectives  515 us (24%)
    reduce_scatter x4, waiting for transfers between devices, advance(): lax.psum_scatter(jnp.einsum('cqr,cqk->rk', rows_here, solved, precision=l...  1590 us
    all_gather x4, blocking collectives, advance(): residual_full = lax.all_gather(residual_part, 'wide', axis=0, tiled=True)  477 us
  transfers between devices with their start and end apart: 5, of which 5 were waited for; matrix products, arithmetic and copies ran while one was open for 0% of the time, Pallas kernels for 0%

commit v1 on v0

--- a/solution.py
+++ b/solution.py
@@ -38,7 +38,15 @@
         )
         residual_part = lax.dynamic_index_in_dim(given_part, own_block, 0, keepdims=False) - reduced
         inverse_rows = lax.dynamic_index_in_dim(block_inverses, block_index, 0, keepdims=False)
-        residual_full = lax.all_gather(residual_part, "wide", axis=0, tiled=True)
+        residual_full = jnp.concatenate(
+            lax.all_to_all(
+                jnp.stack([residual_part for _ in range(lax.axis_size("wide"))], 0),
+                axis_name="wide",
+                split_axis=0,
+                concat_axis=0,
+            ),
+            0,
+        )
         applied = jnp.dot(
             inverse_rows,
             residual_full,

time: 2170 us -> 1840 us (0.85)
  blocking collectives: 515 us -> 52.6 us
  waiting for transfers between devices: 1620 us -> 1690 us
  starting transfers between devices: 0.15 us -> 58.1 us
    all_gather x4 -> x0, blocking collectives: 477 us -> none  [advance(): residual_full = lax.all_gather(residual_part, 'wide', axis=0, tiled=True)]
    all_to_all x0 -> x4, waiting for transfers between devices: none -> 67.7 us  [advance(): lax.all_to_all(jnp.stack([residual_part for _ in range(lax.axis_size('wid...]
    all_to_all x0 -> x4, starting transfers between devices: none -> 58 us  [advance(): lax.all_to_all(jnp.stack([residual_part for _ in range(lax.axis_size('wid...]
  transfers between devices with their start and end apart: 5 -> 9, of which waited for: 5 -> 9; matrix products, arithmetic and copies ran while one was open for 0% -> 0% of each run, Pallas kernels for 0% -> 0%
where the time goes in v1:
time: 1840 us
  waiting for transfers between devices  1690 us (92%)
  starting transfers between devices  58.1 us (3%)
  blocking collectives  52.6 us (3%)
    reduce_scatter x4, waiting for transfers between devices, advance(): lax.psum_scatter(jnp.einsum('cqr,cqk->rk', rows_here, solved, precision=l...  1590 us
    all_to_all x4, waiting for transfers between devices, advance(): lax.all_to_all(jnp.stack([residual_part for _ in range(lax.axis_size('wid...  67.7 us
    all_to_all x4, starting transfers between devices, advance(): lax.all_to_all(jnp.stack([residual_part for _ in range(lax.axis_size('wid...  58 us
    psum x4, blocking collectives, from_root(): return lax.psum(jnp.where(mine, shard, jnp.zeros_like(shard)), axis)  52.6 us
  transfers between devices with their start and end apart: 9, of which 9 were waited for; matrix products, arithmetic and copies ran while one was open for 0% of the time, Pallas kernels for 0%

profile of v1, /device:TPU:8, one launch (start us, length us, event | category | flops | bytes accessed | tf_op | source)
XLA Modules:
  0.0 1838.2 jit_solution(3760407542793656174)
XLA Ops:
  6.5 0.7 reduce-scatter.3.cloned.1.call-update
  7.3 29.7 %reduce-scatter.3.cloned.1.call-done = f32[1,1,1,16,128]{4,3,2,1,0:T(8,128)} async-done(((f32[1,1,4,16,128]{4,3,2,1,0:T(8,128)}), f32[1,1,1,16,128]{4,3,2,1,0:T(8,128)}) %reduce-scatter.3.cloned.1.call-update) | async-done | bytes 8208 | tf_op jit(solution)/shard_map/reduce_scatter | solution.py:21
  36.9 0.7 bitcast_subtract_fusion.1
  37.6 1793.4 %while.15 = (s32[]{:T(128)}, f32[4,16,128]{2,1,0:T(8,128)S(1)}, f32[4,16,1024]{2,1,0:T(8,128)}, f32[1,16,128]{2,1,0:T(8,128)S(1)}, f32[1,4,16,1024]{3,2,1,0:T(8,...) while((s32[]{:T(128)}, f32[4,16,128]{2,1,0:T(8,128)S(1)}, f32[4,16,1024]{2,1,0:T(8,128)}, ...), condition=%wide.region_4.5_spmd, body=%wide.region_1.4_spmd.sunk | while | flops 125835264 | bytes 5177621 | solution.py:60
  37.7 2.7 convolution_bitcast_fusion.2
  40.4 401.7 %reduce-scatter.5.cloned.1.call-done = f32[16,128]{1,0:T(8,128)} async-done(((f32[1024,128]{1,0:T(8,128)}), f32[16,128]{1,0:T(8,128)}) %reduce-scatter.5.cloned.1.call-update) | async-done | bytes 8208 | tf_op jit(solution)/shard_map/while/body/eval_jaxpr/reduce_scatter | solution.py:33
  442.9 0.8 stack.7
  443.7 14.5 all-to-all-start
  458.2 16.5 all-to-all-done
  474.6 1.2 fusion.16
  475.8 13.3 psum.15
  489.3 2.7 convolution_bitcast_fusion.2
  492.0 397.5 %reduce-scatter.5.cloned.1.call-done = f32[16,128]{1,0:T(8,128)} async-done(((f32[1024,128]{1,0:T(8,128)}), f32[16,128]{1,0:T(8,128)}) %reduce-scatter.5.cloned.1.call-update) | async-done | bytes 8208 | tf_op jit(solution)/shard_map/while/body/eval_jaxpr/reduce_scatter | solution.py:33
  890.2 0.8 stack.7
  891.0 14.5 all-to-all-start
  905.6 17.1 all-to-all-done
  922.7 1.2 fusion.16
  923.9 12.8 psum.15
  936.8 2.7 convolution_bitcast_fusion.2
  939.5 397.1 %reduce-scatter.5.cloned.1.call-done = f32[16,128]{1,0:T(8,128)} async-done(((f32[1024,128]{1,0:T(8,128)}), f32[16,128]{1,0:T(8,128)}) %reduce-scatter.5.cloned.1.call-update) | async-done | bytes 8208 | tf_op jit(solution)/shard_map/while/body/eval_jaxpr/reduce_scatter | solution.py:33
  1337.3 0.8 stack.7
  1338.1 14.5 all-to-all-start
  1352.6 17.1 all-to-all-done
  1369.8 1.2 fusion.16
  1371.0 12.9 psum.15
  1384.0 2.7 convolution_bitcast_fusion.2
  1386.7 396.5 %reduce-scatter.5.cloned.1.call-done = f32[16,128]{1,0:T(8,128)} async-done(((f32[1024,128]{1,0:T(8,128)}), f32[16,128]{1,0:T(8,128)}) %reduce-scatter.5.cloned.1.call-update) | async-done | bytes 8208 | tf_op jit(solution)/shard_map/while/body/eval_jaxpr/reduce_scatter | solution.py:33
  1783.9 0.8 stack.7
  1784.8 14.5 all-to-all-start
  1799.2 17.0 all-to-all-done
  1816.2 1.2 fusion.16
  1817.4 13.6 psum.15
  (21 shorter events, 3.7 us)
Async XLA Ops:
  6.5 30.4 %reduce-scatter.3.cloned.1.call-start = ((), (), s32[]{:S(2)}) async-start(), calls=%async_computation.3 | async-start | bytes 40960 | tf_op jit(solution)/shard_map/reduce_scatter | solution.py:21
  7.3 29.7 %copy-start = (f32[1,1,16,128]{3,2,1,0:T(8,128)S(1)}, f32[1,1,16,128]{3,2,1,0:T(8,128)}, u32[]{:S(2)}) copy-start(f32[1,1,16,128]{3,2,1,0:T(8,128)} %param.7) | copy-start | bytes 24580
  37.6 404.5 %reduce-scatter.5.cloned.1.call-start = ((), (), s32[]{:S(2)}) async-start(), calls=%async_computation.4 | async-start | bytes 532480 | tf_op jit(solution)/shard_map/while/body/eval_jaxpr/reduce_scatter | solution.py:33
  443.7 31.0 %all-to-all-start = ((f32[64,16,128]{2,1,0:T(8,128)}), f32[64,16,128]{2,1,0:T(8,128)S(1)}, u32[]{:S(2)}, u32[]{:S(2)}) async-start(f32[64,16,128]{2,1,0:T(8,128)} %stack.7), calls=%async_computation.1 | async-start | bytes 1048576 | tf_op jit(solution)/shard_map/while/body/eval_jaxpr/all_to_all | solution.py:42
  489.2 400.3 %reduce-scatter.5.cloned.1.call-start = ((), (), s32[]{:S(2)}) async-start(), calls=%async_computation.4 | async-start | bytes 532480 | tf_op jit(solution)/shard_map/while/body/eval_jaxpr/reduce_scatter | solution.py:33
  891.0 31.6 %all-to-all-start = ((f32[64,16,128]{2,1,0:T(8,128)}), f32[64,16,128]{2,1,0:T(8,128)S(1)}, u32[]{:S(2)}, u32[]{:S(2)}) async-start(f32[64,16,128]{2,1,0:T(8,128)} %stack.7), calls=%async_computation.1 | async-start | bytes 1048576 | tf_op jit(solution)/shard_map/while/body/eval_jaxpr/all_to_all | solution.py:42
  936.7 399.9 %reduce-scatter.5.cloned.1.call-start = ((), (), s32[]{:S(2)}) async-start(), calls=%async_computation.4 | async-start | bytes 532480 | tf_op jit(solution)/shard_map/while/body/eval_jaxpr/reduce_scatter | solution.py:33
  1338.1 31.7 %all-to-all-start = ((f32[64,16,128]{2,1,0:T(8,128)}), f32[64,16,128]{2,1,0:T(8,128)S(1)}, u32[]{:S(2)}, u32[]{:S(2)}) async-start(f32[64,16,128]{2,1,0:T(8,128)} %stack.7), calls=%async_computation.1 | async-start | bytes 1048576 | tf_op jit(solution)/shard_map/while/body/eval_jaxpr/all_to_all | solution.py:42
  1383.9 399.3 %reduce-scatter.5.cloned.1.call-start = ((), (), s32[]{:S(2)}) async-start(), calls=%async_computation.4 | async-start | bytes 532480 | tf_op jit(solution)/shard_map/while/body/eval_jaxpr/reduce_scatter | solution.py:33
  1784.8 31.4 %all-to-all-start = ((f32[64,16,128]{2,1,0:T(8,128)}), f32[64,16,128]{2,1,0:T(8,128)S(1)}, u32[]{:S(2)}, u32[]{:S(2)}) async-start(f32[64,16,128]{2,1,0:T(8,128)} %stack.7), calls=%async_computation.1 | async-start | bytes 1048576 | tf_op jit(solution)/shard_map/while/body/eval_jaxpr/all_to_all | solution.py:42
Sparse Core Ops, SparseCore 0:
  9.8 27.0 reduce-scatter.2
  41.1 400.9 reduce-scatter.4
  492.7 396.7 reduce-scatter.4
  939.9 396.6 reduce-scatter.4
  1387.1 396.1 reduce-scatter.4
